TPU v7x, 32 devices: a whole 2x2x4 slice. The times are simulated.
32 devices in a mesh: fsdp: 8 (over z, y), tp: 4 (over x, core).
Axes of the slice: x: 2, y: 2, z: 4, core: 2. Of those that a mesh axis runs over, the one named last changes fastest.
Arguments:
- grads: bfloat16 [8, 2, 4096, 2048], P('fsdp', None, 'tp'), may hold values from -144 to 144
- master: float32 [4096, 2048], P('tp', 'fsdp'), may hold values from -0.3125 to 0.3125
- moment: float32 [4096, 2048], P('tp', 'fsdp'), may hold values from -1.5 to 1.5
- second: float32 [4096, 2048], P('tp', 'fsdp'), may hold values from 0.02 to 0.3
- stats: float32 [4, 1024, 1024], P('tp', 'fsdp'), may hold values from -0.05 to 0.35
- basis: float32 [4, 1024, 1024], P('tp', 'fsdp'), may hold values from -0.5 to 1.5
Outputs:
- weights: bfloat16 [4096, 2048], P('tp')
- master_new: float32 [4096, 2048], P('tp', 'fsdp')
- moment_new: float32 [4096, 2048], P('tp', 'fsdp')
- second_new: float32 [4096, 2048], P('tp', 'fsdp')
- stats_new: float32 [4, 1024, 1024], P('tp', 'fsdp')
- basis_new: float32 [4, 1024, 1024], P('tp', 'fsdp')
All inputs are finite; a program needn't handle non-finite values.
Results may differ from a plain program's by a relative error of at most 0.007.
Values may be sent and summed in bfloat16 or wider, within the bound.
A program may use at most 128 MiB of HBM per device.

v0:
```python
import jax
import jax.numpy as jnp
from jax import lax
from jax.sharding import PartitionSpec as P

D = 4096
KVW = 2048
poly_first = 3.4445
poly_second = -4.775
poly_third = 2.0315
bf16 = jnp.bfloat16
f32 = jnp.float32


def exact(a, b):
    return jnp.dot(a, b, precision=lax.Precision.HIGHEST)


def split(a):
    top = a.astype(bf16)
    return (top, (a - top.astype(f32)).astype(bf16))


def three(a, b):
    a_top, a_low = split(a)
    b_top, b_low = split(b)
    mm = lambda u, v: jnp.dot(u, v, preferred_element_type=f32)
    return mm(a_top, b_top) + (mm(a_low, b_top) + mm(a_top, b_low))


def body(grads, master, moment, second, stats, basis):
    n = lax.axis_size("fsdp")
    rows = master.shape[0]
    cols = master.shape[1]
    own_rows = basis[0]
    stat_rows = stats[0]
    whole = lax.all_gather(own_rows.astype(bf16), "fsdp", axis=0, tiled=True)
    local = jnp.sum(grads.astype(f32), axis=(0, 1)).astype(bf16)
    pieces = lax.all_to_all(local, "fsdp", split_axis=1, concat_axis=0, tiled=True)
    summed = jnp.sum(pieces.reshape(n, rows, cols).astype(f32), axis=0)
    squares = jnp.sum(lax.all_gather(jnp.sum(summed * summed).reshape(1), ("fsdp", "tp")))
    ratio = jnp.minimum(1.0, jnp.sqrt(float(D * KVW) / (squares + 1e-06)))
    total = summed.astype(bf16)
    part = jnp.dot(total, total.T, preferred_element_type=f32).astype(bf16)
    strips = lax.all_to_all(part, "fsdp", split_axis=0, concat_axis=0, tiled=True)
    outer = jnp.sum(strips.reshape(n, rows // n, rows).astype(f32), axis=0) * (ratio * ratio)
    stats_new = 0.9 * stat_rows + 0.1 / KVW * outer
    s_top, s_low = split(stats_new)
    power = jnp.dot(s_top, whole, preferred_element_type=f32) + jnp.dot(
        s_low, whole, preferred_element_type=f32
    )
    every = lax.all_gather(power.astype(bf16), "fsdp", axis=0, tiled=True)
    rotated = jnp.dot(whole.T, total, preferred_element_type=f32) * ratio
    moment_new = 0.9 * moment + 0.1 * rotated
    second_new = 0.95 * second + 0.05 * rotated * rotated
    update = moment_new / (jnp.sqrt(second_new) + 1e-08)
    delta = jnp.dot(whole, update.astype(bf16), preferred_element_type=f32)
    master_new = master - 0.01 * (delta + 0.1 * master)
    weights = lax.all_gather(master_new.astype(bf16), "fsdp", axis=1, tiled=True)
    raw = jnp.dot(every.T, every, preferred_element_type=f32)
    diag = lax.broadcasted_iota(jnp.int32, (rows, rows), 0) == lax.broadcasted_iota(
        jnp.int32, (rows, rows), 1
    )
    norm = 1.0 / jnp.sqrt(jnp.sum(jnp.where(diag, raw, 0.0)) + 1e-06)
    gram = raw * (norm * norm)
    current = power * norm
    mixed = jnp.where(diag, poly_first, 0.0) + poly_second * gram + poly_third * three(gram, gram)
    current = three(current, mixed)
    gram = three(mixed, three(mixed, gram))
    product = three(current, gram)
    current = poly_first * current + poly_second * product + poly_third * three(product, gram)
    return (weights, master_new, moment_new, second_new, stats_new[None], current[None])


def solution(mesh):
    in_specs = (
        P("fsdp", None, "tp", None),
        P("tp", "fsdp"),
        P("tp", "fsdp"),
        P("tp", "fsdp"),
        P("tp", "fsdp", None),
        P("tp", "fsdp", None),
    )
    out_specs = (
        P("tp", None),
        P("tp", "fsdp"),
        P("tp", "fsdp"),
        P("tp", "fsdp"),
        P("tp", "fsdp", None),
        P("tp", "fsdp", None),
    )
    return jax.shard_map(body, mesh=mesh, in_specs=in_specs, out_specs=out_specs, check_vma=False)
```

profile of v0, /device:TPU:0, one launch (start us, length us, event | category | flops | bytes accessed | tf_op | source)
XLA Modules:
  0.0 366.2 jit_solution(5923313504358977901)
XLA Ops:
  7.2 8.8 %reduce_sum.57 = bf16[1024,2048]{1,0:T(8,128)(2,1)} reduce(bf16[1,2,1024,2048]{3,2,1,0:T(8,128)(2,1)} %param.6, bf16[]{:T(256)} %constant.16.clone.1), dimensions={0,1}, to_apply=%region_0.0 | reduce | flops 2097152 | bytes 12582914 | tf_op jit(solution)/shard_map/reduce_sum | solution.py:38
  16.0 6.4 %copy.48 = bf16[1024,2048]{0,1:T(8,128)(2,1)} copy(bf16[1024,2048]{1,0:T(8,128)(2,1)} %reduce_sum.57) | data formatting | bytes 8388608 | tf_op jit(solution)/shard_map/reduce_sum | solution.py:38
  22.3 6.4 %copy.49 = bf16[1024,8,256]{2,0,1:T(8,128)(2,1)} copy(bf16[1024,8,256]{0,2,1:T(8,128)(2,1)} %bitcast.79) | data formatting | bytes 8388608 | tf_op jit(solution)/shard_map/all_to_all | solution.py:39
  28.8 100.5 %all_to_all.22 = bf16[1024,8,256]{2,0,1:T(8,128)(2,1)S(1)} all-to-all(bf16[1024,8,256]{2,0,1:T(8,128)(2,1)} %copy.49), channel_id=1, replica_groups=mesh['fsdp'=8,'tp'=4] {'fsdp'}, dimensions={1} | all-to-all | bytes 8388608 | tf_op jit(solution)/shard_map/all_to_all | solution.py:39
  131.9 3.6 all-to-all-start.1
  139.0 84.3 %all-reduce = f32[32]{0:T(128)S(1)} all-reduce(f32[32]{0:T(128)S(1)} %dynamic-update-slice), channel_id=1, replica_groups=mesh['fsdp'=8,'tp'=4] {'fsdp','tp'}, use_global_device_ids=true, to_apply=%add | all-reduce | flops 32 | bytes 256
  225.8 2.5 fusion.1
  230.2 2.5 copy.47
  232.8 2.5 copy.50
  235.3 2.5 copy.52
  237.8 3.8 %fusion.36 = (f32[1024,256]{0,1:T(8,128)}, f32[1024,256]{0,1:T(8,128)}) fusion(f32[1024,256]{0,1:T(8,128)} %copy.50, f32[1024,256]{0,1:T(8,128)} %copy.47, f32[]{:T(128)S(6)} %min.3, bf16[1,1024,1024]{2,1,0:T(8,128)(2,1)S(1)} %copy-done, f32[1024,256]{1,0:T(8,128)S(1)} %convert_reduce_fusion), kind=kOutput, calls=%fused_computation.39 | convolution fusion | flops 539230208 | bytes 7340036 | tf_op jit(solution)/shard_map/dot_general | solution.py:53
  241.7 2.6 copy.55
  245.6 3.6 fusion.71
  249.2 2.6 copy.54
  252.8 26.4 %all-gather.7.cloned.1.call-done = bf16[1024,1024]{1,0:T(8,128)(2,1)} async-done(((bf16[128,1024]{1,0:T(8,128)(2,1)}), bf16[1024,1024]{1,0:T(8,128)(2,1)}) %all-gather.7.cloned.1.call-update) | async-done | bytes 2097168 | tf_op jit(solution)/shard_map/all_gather | solution.py:52
  279.2 7.2 %select_reduce_fusion = (f32[]{:T(128)}, f32[1024,1024]{1,0:T(8,128)}) fusion(bf16[1024,1024]{1,0:T(8,128)(2,1)} %all-gather.7.cloned.1.call-done), kind=kOutput, calls=%fused_computation.8 | convolution fusion | flops 2150629376 | bytes 6291460 | tf_op jit(solution)/shard_map/dot_general | solution.py:60
  287.1 3.3 subtract_convert_fusion.3
  295.2 3.2 subtract_convert_fusion.2
  304.4 2.6 add_add_fusion.1
  307.0 2.3 fusion.54
  309.4 2.3 fusion
  311.7 2.4 add_add_fusion
  317.8 35.5 %all-gather.5.cloned.1.call-done = bf16[1024,2048]{0,1:T(8,128)(2,1)} async-done(((bf16[1024,256]{0,1:T(8,128)(2,1)}), bf16[1024,2048]{0,1:T(8,128)(2,1)}) %all-gather.5.cloned.1.call-update) | async-done | bytes 4194320 | tf_op jit(solution)/shard_map/all_gather | solution.py:59
  353.2 6.4 %copy.53 = bf16[1024,2048]{1,0:T(8,128)(2,1)} copy(bf16[1024,2048]{0,1:T(8,128)(2,1)} %all-gather.5.cloned.1.call-done) | data formatting | bytes 8388608
  (48 shorter events, 26.3 us)
Async XLA Ops:
  131.9 92.8 %all-to-all-start.1 = ((bf16[8,128,1024]{2,1,0:T(8,128)(2,1)}), bf16[8,128,1024]{2,1,0:T(8,128)(2,1)S(1)}, u32[]{:S(2)}, u32[]{:S(2)}) async-start(bf16[8,128,1024]{2,1,0:T(8,128)(2,1)} %bitcast.80), calls=%async_computation.1 | async-start | bytes 4194304 | tf_op jit(solution)/shard_map/all_to_all | solution.py:45
  135.5 90.3 %all-gather.9.cloned.1.call-start = ((), (), s32[]{:S(2)}) async-start(), calls=%async_computation.4 | async-start | bytes 2359296 | tf_op jit(solution)/shard_map/all_gather | solution.py:37
  137.3 141.9 %all-gather.7.cloned.1.call-start = ((), (), s32[]{:S(2)}) async-start(), calls=%async_computation.3 | async-start | bytes 2359296 | tf_op jit(solution)/shard_map/all_gather | solution.py:52
  225.8 2.5 copy-start
  225.8 2.6 copy-start.1
  225.8 2.8 copy-start.4
  230.0 123.2 %all-gather.5.cloned.1.call-start = ((), (), s32[]{:S(2)}) async-start(), calls=%async_computation.2 | async-start | bytes 4718592 | tf_op jit(solution)/shard_map/all_gather | solution.py:59
  241.7 2.6 copy-start.7
  249.2 2.6 copy-start.2
  249.2 2.7 copy-start.5
  292.8 2.4 copy-start.6
  295.2 3.2 copy-start.3
Sparse Core Ops, SparseCore 0:
  139.0 70.8 all-gather.8
  230.1 49.0 all-gather.6
  281.3 71.8 all-gather.4
where the time goes:
time: 367 us; the launch traced here: 366 us
  blocking collectives  185 us (50%)
  waiting for transfers between devices  62 us (17%)
  matrix products  47.8 us (13%)
  local copies, waits for them, and re-layouts  34.4 us (9%)
  other arithmetic  18 us (5%)
  between operations  15.4 us (4%)
  starting transfers between devices  3.91 us (1%)
    all_to_all x1, blocking collectives, body(): lax.all_to_all(local, 'fsdp', split_axis=1, concat_axis=0, tiled=True)  100 us
    unnamed x1, blocking collectives  84.3 us
    all_gather x1, waiting for transfers between devices, body(): lax.all_gather(master_new.astype(bf16), 'fsdp', axis=1, tiled=True)  35.5 us
    dot_general x18, matrix products, three(): mm = lambda u, v: jnp.dot(u, v, preferred_element_type=f32)  27.2 us
    all_gather x1, waiting for transfers between devices, body(): every = lax.all_gather(power.astype(bf16), 'fsdp', axis=0, tiled=True)  26.4 us
    unnamed x25, local copies, waits for them, and re-layouts  21.6 us
    reduce_sum x1, other arithmetic, body(): local = jnp.sum(grads.astype(f32), axis=(0, 1)).astype(bf16)  8.78 us
  transfers between devices with their start and end apart: 4, of which 2 were waited for; matrix products, arithmetic and copies ran while one was open for 18% of the time, Pallas kernels for 0%

commit v1 on v0

--- a/solution.py
+++ b/solution.py
@@ -36,7 +36,10 @@
     stat_rows = stats[0]
     whole = lax.all_gather(own_rows.astype(bf16), "fsdp", axis=0, tiled=True)
     local = jnp.sum(grads.astype(f32), axis=(0, 1)).astype(bf16)
-    pieces = lax.all_to_all(local, "fsdp", split_axis=1, concat_axis=0, tiled=True)
+    devices = lax.axis_size("fsdp")
+    blocks = jnp.stack(jnp.split(local, devices, axis=1), axis=0)
+    blocks = lax.all_to_all(blocks, "fsdp", split_axis=0, concat_axis=0)
+    pieces = jnp.concatenate(blocks, axis=0)
     summed = jnp.sum(pieces.reshape(n, rows, cols).astype(f32), axis=0)
     squares = jnp.sum(lax.all_gather(jnp.sum(summed * summed).reshape(1), ("fsdp", "tp")))
     ratio = jnp.minimum(1.0, jnp.sqrt(float(D * KVW) / (squares + 1e-06)))

time: 367 us -> 364 us (level)
    unnamed x25 -> x26, local copies, waits for them, and re-layouts: 21.6 us -> 29.9 us
    all_to_all x1 -> x0, local copies, waits for them, and re-layouts: 6.42 us -> none  [body(): lax.all_to_all(local, 'fsdp', split_axis=1, concat_axis=0, tiled=True)]
    reduce_sum x1 -> x0, local copies, waits for them, and re-layouts: 6.39 us -> none  [body(): local = jnp.sum(grads.astype(f32), axis=(0, 1)).astype(bf16)]
where the time goes in v1:
time: 364 us; the launch traced here: 363 us
  blocking collectives  185 us (51%)
  waiting for transfers between devices  60.6 us (17%)
  matrix products  49.5 us (14%)
  local copies, waits for them, and re-layouts  31 us (9%)
  other arithmetic  18 us (5%)
  between operations  15.4 us (4%)
  starting transfers between devices  3.91 us (1%)
    all_to_all x1, blocking collectives, body(): blocks = lax.all_to_all(blocks, 'fsdp', split_axis=0, concat_axis=0)  100 us
    unnamed x1, blocking collectives  84.3 us
    all_gather x1, waiting for transfers between devices, body(): lax.all_gather(master_new.astype(bf16), 'fsdp', axis=1, tiled=True)  35.5 us
    unnamed x26, local copies, waits for them, and re-layouts  29.9 us
    dot_general x18, matrix products, three(): mm = lambda u, v: jnp.dot(u, v, preferred_element_type=f32)  27.1 us
    all_gather x1, waiting for transfers between devices, body(): every = lax.all_gather(power.astype(bf16), 'fsdp', axis=0, tiled=True)  25.1 us
    reduce_sum x1, other arithmetic, body(): local = jnp.sum(grads.astype(f32), axis=(0, 1)).astype(bf16)  8.78 us
  transfers between devices with their start and end apart: 4, of which 2 were waited for; matrix products, arithmetic and copies ran while one was open for 18% of the time, Pallas kernels for 0%

profile of v1, /device:TPU:0, one launch (start us, length us, event | category | flops | bytes accessed | tf_op | source)
XLA Modules:
  0.0 363.0 jit_solution(7728459106254674096)
XLA Ops:
  7.2 8.8 %reduce_sum.57 = bf16[1024,2048]{1,0:T(8,128)(2,1)} reduce(bf16[1,2,1024,2048]{3,2,1,0:T(8,128)(2,1)} %param.6, bf16[]{:T(256)} %constant.16.clone.1), dimensions={0,1}, to_apply=%region_0.0 | reduce | flops 2097152 | bytes 12582914 | tf_op jit(solution)/shard_map/reduce_sum | solution.py:38
  24.6 100.3 %all_to_all.14 = bf16[8,1024,256]{2,1,0:T(8,128)(2,1)S(1)} all-to-all(bf16[8,1024,256]{2,1,0:T(8,128)(2,1)S(1)} %fusion.37), channel_id=1, replica_groups=mesh['fsdp'=8,'tp'=4] {'fsdp'}, dimensions={0} | all-to-all | bytes 8388608 | tf_op jit(solution)/shard_map/all_to_all | solution.py:41
  127.5 3.6 all-to-all-start.1
  134.7 84.3 %all-reduce = f32[32]{0:T(128)S(1)} all-reduce(f32[32]{0:T(128)S(1)} %dynamic-update-slice), channel_id=1, replica_groups=mesh['fsdp'=8,'tp'=4] {'fsdp','tp'}, use_global_device_ids=true, to_apply=%add | all-reduce | flops 32 | bytes 256
  221.4 2.5 fusion.1
  224.0 2.6 fusion.80
  226.9 2.5 copy.20
  229.4 2.5 copy.21
  231.9 2.5 copy.23
  234.5 3.8 %fusion.36 = (f32[1024,256]{0,1:T(8,128)}, f32[1024,256]{0,1:T(8,128)}) fusion(f32[1024,256]{0,1:T(8,128)} %copy.21, f32[1024,256]{0,1:T(8,128)} %copy.20, f32[]{:T(128)S(6)} %min.3, bf16[1,1024,1024]{2,1,0:T(8,128)(2,1)S(1)} %copy-done, f32[1024,256]{1,0:T(8,128)S(1)} %convert_reduce_fusion), kind=kOutput, calls=%fused_computation.39 | convolution fusion | flops 539230208 | bytes 7340036 | tf_op jit(solution)/shard_map/dot_general | solution.py:56
  238.3 2.5 copy.26
  240.8 2.5 copy.27
  243.4 4.1 %fusion.79 = (bf16[1024,256]{0,1:T(8,128)(2,1)}, f32[1024,256]{0,1:T(8,128)}) fusion(f32[1024,256]{0,1:T(8,128)} %copy.23, bf16[1,1024,1024]{2,1,0:T(8,128)(2,1)S(1)} %copy-done, f32[1024,256]{0,1:T(8,128)} %get-tuple-element.23, f32[1024,256]{0,1:T(8,128)} %get-tuple-element.22), kind=kOutput, calls=%fused_computation.99 | convolution fusion | flops 538968064 | bytes 6815744 | tf_op jit(solution)/shard_map/dot_general | solution.py:60
  247.4 2.5 copy.25
  250.9 25.1 %all-gather.7.cloned.1.call-done = bf16[1024,1024]{1,0:T(8,128)(2,1)} async-done(((bf16[128,1024]{1,0:T(8,128)(2,1)}), bf16[1024,1024]{1,0:T(8,128)(2,1)}) %all-gather.7.cloned.1.call-update) | async-done | bytes 2097168 | tf_op jit(solution)/shard_map/all_gather | solution.py:55
  276.0 7.2 %select_reduce_fusion = (f32[]{:T(128)}, f32[1024,1024]{1,0:T(8,128)}) fusion(bf16[1024,1024]{1,0:T(8,128)(2,1)} %all-gather.7.cloned.1.call-done), kind=kOutput, calls=%fused_computation.8 | convolution fusion | flops 2150629376 | bytes 6291460 | tf_op jit(solution)/shard_map/dot_general | solution.py:63
  283.9 3.3 subtract_convert_fusion.3
  292.0 3.2 subtract_convert_fusion.2
  301.2 2.5 add_add_fusion.1
  303.8 2.3 fusion.62
  306.1 2.4 fusion
  308.5 2.4 add_add_fusion
  314.5 35.5 %all-gather.5.cloned.1.call-done = bf16[1024,2048]{0,1:T(8,128)(2,1)} async-done(((bf16[1024,256]{0,1:T(8,128)(2,1)}), bf16[1024,2048]{0,1:T(8,128)(2,1)}) %all-gather.5.cloned.1.call-update) | async-done | bytes 4194320 | tf_op jit(solution)/shard_map/all_gather | solution.py:62
  350.0 6.4 %copy.24 = bf16[1024,2048]{1,0:T(8,128)(2,1)} copy(bf16[1024,2048]{0,1:T(8,128)(2,1)} %all-gather.5.cloned.1.call-done) | data formatting | bytes 8388608
  (48 shorter events, 32.0 us)
Async XLA Ops:
  127.5 92.8 %all-to-all-start.1 = ((bf16[8,128,1024]{2,1,0:T(8,128)(2,1)}), bf16[8,128,1024]{2,1,0:T(8,128)(2,1)S(1)}, u32[]{:S(2)}, u32[]{:S(2)}) async-start(bf16[8,128,1024]{2,1,0:T(8,128)(2,1)} %bitcast.110), calls=%async_computation.1 | async-start | bytes 4194304 | tf_op jit(solution)/shard_map/all_to_all | solution.py:48
  131.1 90.3 %all-gather.9.cloned.1.call-start = ((), (), s32[]{:S(2)}) async-start(), calls=%async_computation.4 | async-start | bytes 2359296 | tf_op jit(solution)/shard_map/all_gather | solution.py:37
  133.0 143.0 %all-gather.7.cloned.1.call-start = ((), (), s32[]{:S(2)}) async-start(), calls=%async_computation.3 | async-start | bytes 2359296 | tf_op jit(solution)/shard_map/all_gather | solution.py:55
  221.4 2.5 copy-start
  226.6 123.4 %all-gather.5.cloned.1.call-start = ((), (), s32[]{:S(2)}) async-start(), calls=%async_computation.2 | async-start | bytes 4718592 | tf_op jit(solution)/shard_map/all_gather | solution.py:62
  243.4 6.6 %copy-start.1 = (f32[128,1024]{1,0:T(8,128)S(1)}, f32[128,1024]{1,0:T(8,128)}, u32[]{:S(2)}) copy-start(f32[128,1024]{1,0:T(8,128)} %convert_reduce_fusion.1) | copy-start | bytes 1572868
  243.4 6.6 %copy-start.3 = (f32[1,128,1024]{2,1,0:T(8,128)S(1)}, f32[1,128,1024]{2,1,0:T(8,128)}, u32[]{:S(2)}) copy-start(f32[1,128,1024]{2,1,0:T(8,128)} %param.10) | copy-start | bytes 1572868
  289.6 2.4 copy-start.4
  292.0 3.2 copy-start.2
Sparse Core Ops, SparseCore 0:
  134.7 70.8 all-gather.8
  226.8 49.1 all-gather.6
  278.1 71.8 all-gather.4
